TPU v7x, 32 devices: a whole 2x2x4 slice. The times are simulated.
32 devices in a mesh: section: 2 (over y), expert: 8 (over z, x), dp: 2 (over core).
Axes of the slice: x: 2, y: 2, z: 4, core: 2. Of those that a mesh axis runs over, the one named last changes fastest.
Arguments:
- tokens_in: bfloat16 [8, 256, 2048], P(None, ('expert', 'dp')), may hold values from -6 to 6
- cotangent: bfloat16 [8, 256, 2048], P(None, ('expert', 'dp')), may hold values from -4 to 4
- routes: int32 [2, 8, 256, 8], P('section', None, ('expert', 'dp')), may hold values from 0 to 15, all different within a row; in each aligned block of 16 rows (0 to 15, 16 to 31, ..., all dimensions but the last counted through in order) at most 10 rows name the same one
- router_weights: float32 [2, 8, 256, 8], P('section', None, ('expert', 'dp')), may hold values from 0.1 to 0.6
- norm_gain: float32 [2, 2048], P('section'), may hold values from 0.25 to 1.75
- w_gate: bfloat16 [2, 16, 2048, 512], P('section', 'expert'), may hold values from -0.125 to 0.125
- w_up: bfloat16 [2, 16, 2048, 512], P('section', 'expert'), may hold values from -0.125 to 0.125
- w_down: bfloat16 [2, 16, 512, 2048], P('section', 'expert'), may hold values from -0.25 to 0.25
Outputs:
- layer_out: bfloat16 [2, 8, 256, 2048], P('section', None, ('expert', 'dp'))
- input_grad: bfloat16 [2, 8, 256, 2048], P('section', None, ('expert', 'dp'))
- grad_gate: bfloat16 [2, 16, 2048, 512], P('section', 'expert', 'dp')
- grad_up: bfloat16 [2, 16, 2048, 512], P('section', 'expert', 'dp')
- grad_down: bfloat16 [2, 16, 512, 2048], P('section', 'expert', 'dp')
Inputs may be any that keep to these rules, and one draw needn't show every extreme that they name: `routes`: each row names 8 different experts. In each aligned block of 16 rows (the tokens of one device for one layer and one micro-batch) no expert is named by more than 10 rows, and in some blocks one is named by exactly 10.
All inputs are finite; a program needn't handle non-finite values.
Results may differ from a plain program's by a relative error of at most 0.022.
Values may be sent and summed in bfloat16 or wider, within the bound.
A program may use at most 128 MiB of HBM per device.

v0:
```python
import jax
import jax.numpy as jnp
from jax import lax
from jax.sharding import PartitionSpec as P

epsilon = 1e-06


def from_behind(block, axis, distance):
    devices = range(lax.axis_size(axis))
    route = [(i - distance, i) for i in devices if i - distance in devices]
    return lax.ppermute(block, axis, route)


def normalize(hidden, gain_row):
    widened = hidden.astype(jnp.float32)
    inv_rms = lax.rsqrt(jnp.mean(widened * widened, axis=-1, keepdims=True) + epsilon)
    return ((widened * inv_rms * gain_row).astype(jnp.bfloat16), widened, inv_rms)


def routing_tables(route_ids, route_weights, capacity, experts):
    micro_count, token_rows, top_count = route_ids.shape
    assigned = token_rows * top_count
    flat_ids = route_ids.reshape(micro_count, assigned)
    labels = jnp.arange(experts, dtype=jnp.int32)
    onehot = (flat_ids[:, :, None] == labels[None, None, :]).astype(jnp.int32)
    earlier = jnp.cumsum(onehot, axis=1) - onehot
    position = jnp.sum(earlier * onehot, axis=2)
    target = flat_ids * capacity + position
    places = jnp.arange(experts * capacity, dtype=jnp.int32)
    matched = (target[:, None, :] == places[None, :, None]).reshape(
        micro_count, experts * capacity, token_rows, top_count
    )
    selector = jnp.any(matched, axis=3).astype(jnp.bfloat16)
    weighted = jnp.sum(jnp.where(matched, route_weights[:, None, :, :], 0.0), axis=3)
    return (selector, weighted)


def expert_forward(rows_in, gate_w, up_w, down_w):
    gate_pre = jnp.einsum("erx,exf->erf", rows_in, gate_w, preferred_element_type=jnp.float32)
    up_pre = jnp.einsum("erx,exf->erf", rows_in, up_w, preferred_element_type=jnp.float32)
    act_value = (jax.nn.silu(gate_pre) * up_pre).astype(jnp.bfloat16)
    produced = jnp.einsum(
        "erf,efx->erx", act_value, down_w, preferred_element_type=jnp.float32
    ).astype(jnp.bfloat16)
    return (produced, gate_pre, up_pre)


def expert_backward(out_grad, gate_pre, up_pre, gate_w, up_w, down_w):
    act_grad = jnp.einsum("erx,efx->erf", out_grad, down_w, preferred_element_type=jnp.float32)
    sigmoid_g = jax.nn.sigmoid(gate_pre)
    up_grad = (act_grad * gate_pre * sigmoid_g).astype(jnp.bfloat16)
    gate_grad = (act_grad * up_pre * sigmoid_g * (1.0 + gate_pre * (1.0 - sigmoid_g))).astype(
        jnp.bfloat16
    )
    row_grad = jnp.einsum("erf,exf->erx", gate_grad, gate_w, preferred_element_type=jnp.float32)
    row_grad = row_grad + jnp.einsum(
        "erf,exf->erx", up_grad, up_w, preferred_element_type=jnp.float32
    )
    return (row_grad.astype(jnp.bfloat16), gate_grad, up_grad)


def keep_slice(stored, new_value, at_index, is_valid):
    previous = lax.dynamic_index_in_dim(stored, at_index, 0, keepdims=False)
    return lax.dynamic_update_index_in_dim(
        stored, jnp.where(is_valid, new_value, previous), at_index, 0
    )


def round_part(partial_value):
    return lax.optimization_barrier(partial_value.astype(jnp.bfloat16)).astype(jnp.float32)


def send_out(buffer):
    return lax.all_to_all(buffer, "expert", split_axis=0, concat_axis=1, tiled=True)


def send_back(buffer):
    return lax.all_to_all(buffer, "expert", split_axis=1, concat_axis=0, tiled=True)


def on_device(tokens_in, cotangent, routes, router_weights, norm_gain, w_gate, w_up, w_down):
    micro_count, token_rows, model_width = tokens_in.shape
    top_count = routes.shape[3]
    hidden_units = w_gate.shape[3]
    section_count = lax.axis_size("section")
    expert_count = lax.axis_size("expert")
    held_count = w_gate.shape[1]
    experts = held_count * expert_count
    capacity = min(token_rows, 5 * token_rows * top_count // (4 * experts))
    slot_count = experts * capacity
    section_id = lax.axis_index("section")
    selector, weighted = routing_tables(routes[0], router_weights[0], capacity, experts)
    slot_weight = jnp.sum(weighted, axis=2)
    gain_row = norm_gain[0]
    gate_local = w_gate[0]
    up_local = w_up[0]
    down_local = w_down[0]
    expert_rows = expert_count * capacity
    tick_count = section_count + micro_count - 1

    def forward_tick(tick_id, loop_state):
        incoming, inputs_kept, rows_kept, gate_kept, up_kept, outputs_kept = loop_state
        micro_id = tick_id - section_id
        is_valid = jnp.logical_and(micro_id >= 0, micro_id < micro_count)
        clipped = jnp.clip(micro_id, 0, micro_count - 1)
        fresh_in = lax.dynamic_index_in_dim(tokens_in, clipped, 0, keepdims=False)
        hidden = jnp.where(section_id == 0, fresh_in, incoming)
        normed, widened, inv_rms = normalize(hidden, gain_row)
        chooser = lax.dynamic_index_in_dim(selector, clipped, 0, keepdims=False)
        spread = jnp.dot(chooser, normed, preferred_element_type=jnp.float32).astype(jnp.bfloat16)
        arrived = send_out(spread.reshape(experts, capacity, model_width))

        def forward_compute(rows_in):
            return expert_forward(rows_in, gate_local, up_local, down_local)

        def forward_skipped(rows_in):
            return (
                jnp.zeros((held_count, expert_rows, model_width), jnp.bfloat16),
                jnp.zeros((held_count, expert_rows, hidden_units), jnp.float32),
                jnp.zeros((held_count, expert_rows, hidden_units), jnp.float32),
            )

        produced, gate_value, up_value = lax.cond(
            is_valid, forward_compute, forward_skipped, arrived
        )
        returned = send_back(produced).reshape(slot_count, model_width)
        mix_table = lax.dynamic_index_in_dim(weighted, clipped, 0, keepdims=False)
        mixed_sum = widened + jnp.dot(
            mix_table.T,
            returned.astype(jnp.float32),
            precision=lax.Precision.HIGHEST,
            preferred_element_type=jnp.float32,
        )
        output = mixed_sum.astype(jnp.bfloat16)
        inputs_kept = keep_slice(inputs_kept, hidden, clipped, is_valid)
        rows_kept = keep_slice(rows_kept, arrived, clipped, is_valid)
        gate_kept = keep_slice(gate_kept, gate_value, clipped, is_valid)
        up_kept = keep_slice(up_kept, up_value, clipped, is_valid)
        outputs_kept = keep_slice(outputs_kept, output, clipped, is_valid)
        outgoing = from_behind(output, "section", 1)
        return (outgoing, inputs_kept, rows_kept, gate_kept, up_kept, outputs_kept)

    start_state = (
        jnp.zeros((token_rows, model_width), jnp.bfloat16),
        jnp.zeros((micro_count, token_rows, model_width), jnp.bfloat16),
        jnp.zeros((micro_count, held_count, expert_rows, model_width), jnp.bfloat16),
        jnp.zeros((micro_count, held_count, expert_rows, hidden_units), jnp.float32),
        jnp.zeros((micro_count, held_count, expert_rows, hidden_units), jnp.float32),
        jnp.zeros((micro_count, token_rows, model_width), jnp.bfloat16),
    )
    forward_state = lax.fori_loop(0, tick_count, forward_tick, start_state)
    inputs_kept = forward_state[1]
    rows_kept = forward_state[2]
    gate_kept = forward_state[3]
    up_kept = forward_state[4]
    outputs_kept = forward_state[5]

    def backward_tick(tick_id, loop_state):
        incoming, out_kept, gate_grads_kept, up_grads_kept, grads_kept = loop_state
        micro_id = tick_id - (section_count - 1 - section_id)
        is_valid = jnp.logical_and(micro_id >= 0, micro_id < micro_count)
        clipped = jnp.clip(micro_id, 0, micro_count - 1)
        fresh_in = lax.dynamic_index_in_dim(cotangent, clipped, 0, keepdims=False)
        grad_out = jnp.where(section_id == section_count - 1, fresh_in, incoming)
        chooser = lax.dynamic_index_in_dim(selector, clipped, 0, keepdims=False)
        gathered = jnp.dot(chooser, grad_out, preferred_element_type=jnp.float32)
        weight_col = lax.dynamic_index_in_dim(slot_weight, clipped, 0, keepdims=False)
        out_grad = (weight_col[:, None] * gathered).astype(jnp.bfloat16)
        arrived = send_out(out_grad.reshape(experts, capacity, model_width))
        gate_value = lax.dynamic_index_in_dim(gate_kept, clipped, 0, keepdims=False)
        up_value = lax.dynamic_index_in_dim(up_kept, clipped, 0, keepdims=False)

        def backward_compute(operands):
            return expert_backward(
                operands[0], operands[1], operands[2], gate_local, up_local, down_local
            )

        def backward_skipped(operands):
            return (
                jnp.zeros((held_count, expert_rows, model_width), jnp.bfloat16),
                jnp.zeros((held_count, expert_rows, hidden_units), jnp.bfloat16),
                jnp.zeros((held_count, expert_rows, hidden_units), jnp.bfloat16),
            )

        row_grad, gate_grad, up_grad = lax.cond(
            is_valid, backward_compute, backward_skipped, (arrived, gate_value, up_value)
        )
        backed = send_back(row_grad).reshape(slot_count, model_width)
        dnormed = jnp.dot(chooser.T, backed, preferred_element_type=jnp.float32)
        hidden = lax.dynamic_index_in_dim(inputs_kept, clipped, 0, keepdims=False)
        widened = hidden.astype(jnp.float32)
        inv_rms = lax.rsqrt(jnp.mean(widened * widened, axis=-1, keepdims=True) + epsilon)
        unit_rows = widened * inv_rms
        scaled = dnormed * gain_row
        dhidden = grad_out.astype(jnp.float32) + inv_rms * (
            scaled - unit_rows * jnp.mean(scaled * unit_rows, axis=-1, keepdims=True)
        )
        result = dhidden.astype(jnp.bfloat16)
        out_kept = keep_slice(out_kept, arrived, clipped, is_valid)
        gate_grads_kept = keep_slice(gate_grads_kept, gate_grad, clipped, is_valid)
        up_grads_kept = keep_slice(up_grads_kept, up_grad, clipped, is_valid)
        grads_kept = keep_slice(grads_kept, result, clipped, is_valid)
        outgoing = from_behind(result, "section", -1)
        return (outgoing, out_kept, gate_grads_kept, up_grads_kept, grads_kept)

    back_start = (
        jnp.zeros((token_rows, model_width), jnp.bfloat16),
        jnp.zeros((micro_count, held_count, expert_rows, model_width), jnp.bfloat16),
        jnp.zeros((micro_count, held_count, expert_rows, hidden_units), jnp.bfloat16),
        jnp.zeros((micro_count, held_count, expert_rows, hidden_units), jnp.bfloat16),
        jnp.zeros((micro_count, token_rows, model_width), jnp.bfloat16),
    )
    back_state = lax.fori_loop(0, tick_count, backward_tick, back_start)
    out_kept = back_state[1]
    gate_grads_kept = back_state[2]
    up_grads_kept = back_state[3]
    grads_kept = back_state[4]
    act_all = (jax.nn.silu(gate_kept) * up_kept).astype(jnp.bfloat16)
    part_gate = jnp.einsum(
        "merx,merf->exf", rows_kept, gate_grads_kept, preferred_element_type=jnp.float32
    )
    part_up = jnp.einsum(
        "merx,merf->exf", rows_kept, up_grads_kept, preferred_element_type=jnp.float32
    )
    part_down = jnp.einsum("merf,merx->efx", act_all, out_kept, preferred_element_type=jnp.float32)
    summed = (
        lax.psum_scatter(
            round_part(part_gate).astype(jnp.bfloat16), "dp", scatter_dimension=1, tiled=True
        ).astype(jnp.float32),
        lax.psum_scatter(
            round_part(part_up).astype(jnp.bfloat16), "dp", scatter_dimension=1, tiled=True
        ).astype(jnp.float32),
        lax.psum_scatter(
            round_part(part_down).astype(jnp.bfloat16), "dp", scatter_dimension=1, tiled=True
        ).astype(jnp.float32),
    )
    grad_gate = summed[0].astype(jnp.bfloat16)
    grad_up = summed[1].astype(jnp.bfloat16)
    grad_down = summed[2].astype(jnp.bfloat16)
    return (outputs_kept[None], grads_kept[None], grad_gate[None], grad_up[None], grad_down[None])


def solution(mesh):
    placed = (
        P(None, ("expert", "dp"), None),
        P(None, ("expert", "dp"), None),
        P("section", None, ("expert", "dp"), None),
        P("section", None, ("expert", "dp"), None),
        P("section", None),
        P("section", "expert", None, None),
        P("section", "expert", None, None),
        P("section", "expert", None, None),
    )
    return jax.shard_map(
        on_device,
        mesh=mesh,
        in_specs=placed,
        out_specs=(
            P("section", None, ("expert", "dp"), None),
            P("section", None, ("expert", "dp"), None),
            P("section", "expert", "dp", None),
            P("section", "expert", "dp", None),
            P("section", "expert", "dp", None),
        ),
        check_vma=False,
    )
```

profile of v0, /device:TPU:0, one launch (start us, length us, event | category | flops | bytes accessed | tf_op | source)
XLA Modules:
  0.0 1394.0 jit_solution(1228539044011185446)
XLA Ops:
  21.6 651.4 %while.47 = (s32[]{:T(128)}, bf16[16,2048]{1,0:T(8,128)(2,1)S(1)}, bf16[8,16,2048]{2,1,0:T(8,128)(2,1)}, bf16[8,2,80,2048]{3,2,0,1:T(8,128)(2,1)}, f32[8,2,80,51...) while((s32[]{:T(128)}, bf16[16,2048]{1,0:T(8,128)(2,1)S(1)}, ...), condition=%wide.region_8.9_spmd, body=%wide.region_4.0_spmd.sunk | while | flops 1082097664 | bytes 73764016 | solution.py:152
  34.9 23.8 %all-to-all-done = bf16[16,10,2048]{2,1,0:T(8,128)(2,1)S(1)} async-done(((bf16[16,10,2048]{2,1,0:T(8,128)(2,1)}), bf16[16,10,2048]{2,1,0:T(8,128)(2,1)S(1)}, u32[]{:S(2)}, u32[]{:S(2)}) %all-to-all-start) | async-done | bytes 655392 | tf_op jit(solution)/shard_map/while/body/eval_jaxpr/all_to_all | solution.py:75
  105.2 24.0 %all-to-all-done = bf16[16,10,2048]{2,1,0:T(8,128)(2,1)S(1)} async-done(((bf16[16,10,2048]{2,1,0:T(8,128)(2,1)}), bf16[16,10,2048]{2,1,0:T(8,128)(2,1)S(1)}, u32[]{:S(2)}, u32[]{:S(2)}) %all-to-all-start) | async-done | bytes 655392 | tf_op jit(solution)/shard_map/while/body/eval_jaxpr/all_to_all | solution.py:75
  177.9 23.7 %all-to-all-done = bf16[16,10,2048]{2,1,0:T(8,128)(2,1)S(1)} async-done(((bf16[16,10,2048]{2,1,0:T(8,128)(2,1)}), bf16[16,10,2048]{2,1,0:T(8,128)(2,1)S(1)}, u32[]{:S(2)}, u32[]{:S(2)}) %all-to-all-start) | async-done | bytes 655392 | tf_op jit(solution)/shard_map/while/body/eval_jaxpr/all_to_all | solution.py:75
  220.7 12.9 all-to-all-done.1
  250.1 23.7 %all-to-all-done = bf16[16,10,2048]{2,1,0:T(8,128)(2,1)S(1)} async-done(((bf16[16,10,2048]{2,1,0:T(8,128)(2,1)}), bf16[16,10,2048]{2,1,0:T(8,128)(2,1)S(1)}, u32[]{:S(2)}, u32[]{:S(2)}) %all-to-all-start) | async-done | bytes 655392 | tf_op jit(solution)/shard_map/while/body/eval_jaxpr/all_to_all | solution.py:75
  322.2 23.7 %all-to-all-done = bf16[16,10,2048]{2,1,0:T(8,128)(2,1)S(1)} async-done(((bf16[16,10,2048]{2,1,0:T(8,128)(2,1)}), bf16[16,10,2048]{2,1,0:T(8,128)(2,1)S(1)}, u32[]{:S(2)}, u32[]{:S(2)}) %all-to-all-start) | async-done | bytes 655392 | tf_op jit(solution)/shard_map/while/body/eval_jaxpr/all_to_all | solution.py:75
  394.3 23.7 %all-to-all-done = bf16[16,10,2048]{2,1,0:T(8,128)(2,1)S(1)} async-done(((bf16[16,10,2048]{2,1,0:T(8,128)(2,1)}), bf16[16,10,2048]{2,1,0:T(8,128)(2,1)S(1)}, u32[]{:S(2)}, u32[]{:S(2)}) %all-to-all-start) | async-done | bytes 655392 | tf_op jit(solution)/shard_map/while/body/eval_jaxpr/all_to_all | solution.py:75
  466.5 23.7 %all-to-all-done = bf16[16,10,2048]{2,1,0:T(8,128)(2,1)S(1)} async-done(((bf16[16,10,2048]{2,1,0:T(8,128)(2,1)}), bf16[16,10,2048]{2,1,0:T(8,128)(2,1)S(1)}, u32[]{:S(2)}, u32[]{:S(2)}) %all-to-all-start) | async-done | bytes 655392 | tf_op jit(solution)/shard_map/while/body/eval_jaxpr/all_to_all | solution.py:75
  538.6 23.7 %all-to-all-done = bf16[16,10,2048]{2,1,0:T(8,128)(2,1)S(1)} async-done(((bf16[16,10,2048]{2,1,0:T(8,128)(2,1)}), bf16[16,10,2048]{2,1,0:T(8,128)(2,1)S(1)}, u32[]{:S(2)}, u32[]{:S(2)}) %all-to-all-start) | async-done | bytes 655392 | tf_op jit(solution)/shard_map/while/body/eval_jaxpr/all_to_all | solution.py:75
  581.4 12.9 all-to-all-done.1
  610.8 23.7 %all-to-all-done = bf16[16,10,2048]{2,1,0:T(8,128)(2,1)S(1)} async-done(((bf16[16,10,2048]{2,1,0:T(8,128)(2,1)}), bf16[16,10,2048]{2,1,0:T(8,128)(2,1)S(1)}, u32[]{:S(2)}, u32[]{:S(2)}) %all-to-all-start) | async-done | bytes 655392 | tf_op jit(solution)/shard_map/while/body/eval_jaxpr/all_to_all | solution.py:75
  646.5 12.9 all-to-all-done.1
  678.5 657.6 %while.48 = (s32[]{:T(128)}, bf16[16,2048]{1,0:T(8,128)(2,1)S(1)}, bf16[8,2,80,2048]{3,2,1,0:T(8,128)(2,1)}, bf16[8,2,80,512]{3,2,0,1:T(8,128)(2,1)}, bf16[8,2,8...) while((s32[]{:T(128)}, bf16[16,2048]{1,0:T(8,128)(2,1)S(1)}, ...), condition=%wide.region_15.16_spmd, body=%wide.region_10.15_spmd.sunk | while | flops 1031094272 | bytes 74154120 | solution.py:214
  686.7 23.2 %all-to-all-done.2 = bf16[16,10,2048]{2,1,0:T(8,128)(2,1)S(1)} async-done(((bf16[16,10,2048]{2,1,0:T(8,128)(2,1)}), bf16[16,10,2048]{2,1,0:T(8,128)(2,1)S(1)}, u32[]{:S(2)}, u32[]{:S(2)}) %all-to-all-start.2) | async-done | bytes 655392 | tf_op jit(solution)/shard_map/while/body/eval_jaxpr/all_to_all | solution.py:75
  759.4 23.4 %all-to-all-done.2 = bf16[16,10,2048]{2,1,0:T(8,128)(2,1)S(1)} async-done(((bf16[16,10,2048]{2,1,0:T(8,128)(2,1)}), bf16[16,10,2048]{2,1,0:T(8,128)(2,1)S(1)}, u32[]{:S(2)}, u32[]{:S(2)}) %all-to-all-start.2) | async-done | bytes 655392 | tf_op jit(solution)/shard_map/while/body/eval_jaxpr/all_to_all | solution.py:75
  833.0 22.9 %all-to-all-done.2 = bf16[16,10,2048]{2,1,0:T(8,128)(2,1)S(1)} async-done(((bf16[16,10,2048]{2,1,0:T(8,128)(2,1)}), bf16[16,10,2048]{2,1,0:T(8,128)(2,1)S(1)}, u32[]{:S(2)}, u32[]{:S(2)}) %all-to-all-start.2) | async-done | bytes 655392 | tf_op jit(solution)/shard_map/while/body/eval_jaxpr/all_to_all | solution.py:75
  906.1 22.9 %all-to-all-done.2 = bf16[16,10,2048]{2,1,0:T(8,128)(2,1)S(1)} async-done(((bf16[16,10,2048]{2,1,0:T(8,128)(2,1)}), bf16[16,10,2048]{2,1,0:T(8,128)(2,1)S(1)}, u32[]{:S(2)}, u32[]{:S(2)}) %all-to-all-start.2) | async-done | bytes 655392 | tf_op jit(solution)/shard_map/while/body/eval_jaxpr/all_to_all | solution.py:75
  979.1 22.9 %all-to-all-done.2 = bf16[16,10,2048]{2,1,0:T(8,128)(2,1)S(1)} async-done(((bf16[16,10,2048]{2,1,0:T(8,128)(2,1)}), bf16[16,10,2048]{2,1,0:T(8,128)(2,1)S(1)}, u32[]{:S(2)}, u32[]{:S(2)}) %all-to-all-start.2) | async-done | bytes 655392 | tf_op jit(solution)/shard_map/while/body/eval_jaxpr/all_to_all | solution.py:75
  1052.1 22.9 %all-to-all-done.2 = bf16[16,10,2048]{2,1,0:T(8,128)(2,1)S(1)} async-done(((bf16[16,10,2048]{2,1,0:T(8,128)(2,1)}), bf16[16,10,2048]{2,1,0:T(8,128)(2,1)S(1)}, u32[]{:S(2)}, u32[]{:S(2)}) %all-to-all-start.2) | async-done | bytes 655392 | tf_op jit(solution)/shard_map/while/body/eval_jaxpr/all_to_all | solution.py:75
  1125.2 22.9 %all-to-all-done.2 = bf16[16,10,2048]{2,1,0:T(8,128)(2,1)S(1)} async-done(((bf16[16,10,2048]{2,1,0:T(8,128)(2,1)}), bf16[16,10,2048]{2,1,0:T(8,128)(2,1)S(1)}, u32[]{:S(2)}, u32[]{:S(2)}) %all-to-all-start.2) | async-done | bytes 655392 | tf_op jit(solution)/shard_map/while/body/eval_jaxpr/all_to_all | solution.py:75
  1198.2 22.9 %all-to-all-done.2 = bf16[16,10,2048]{2,1,0:T(8,128)(2,1)S(1)} async-done(((bf16[16,10,2048]{2,1,0:T(8,128)(2,1)}), bf16[16,10,2048]{2,1,0:T(8,128)(2,1)S(1)}, u32[]{:S(2)}, u32[]{:S(2)}) %all-to-all-start.2) | async-done | bytes 655392 | tf_op jit(solution)/shard_map/while/body/eval_jaxpr/all_to_all | solution.py:75
  1271.3 22.9 %all-to-all-done.2 = bf16[16,10,2048]{2,1,0:T(8,128)(2,1)S(1)} async-done(((bf16[16,10,2048]{2,1,0:T(8,128)(2,1)}), bf16[16,10,2048]{2,1,0:T(8,128)(2,1)S(1)}, u32[]{:S(2)}, u32[]{:S(2)}) %all-to-all-start.2) | async-done | bytes 655392 | tf_op jit(solution)/shard_map/while/body/eval_jaxpr/all_to_all | solution.py:75
  1371.2 16.2 %reduce-scatter.8.cloned.1.call-done = bf16[2,256,2048]{2,1,0:T(8,128)(2,1)} async-done(((bf16[2,512,2048]{2,1,0:T(8,128)(2,1)}), bf16[2,256,2048]{2,1,0:T(8,128)(2,1)}) %reduce-scatter.8.cloned.1.call-update) | async-done | bytes 2097168 | tf_op jit(solution)/shard_map/reduce_scatter | solution.py:234
  (629 shorter events, 1056.0 us)
Async XLA Ops:
  7.2 1357.9 %reduce-scatter.6.cloned.1.call-start = ((), (), s32[]{:S(2)}) async-start(), calls=%async_computation.8 | async-start | bytes 6291456 | tf_op jit(solution)/shard_map/reduce_scatter | solution.py:231
  25.7 33.0 %all-to-all-start = ((bf16[16,10,2048]{2,1,0:T(8,128)(2,1)}), bf16[16,10,2048]{2,1,0:T(8,128)(2,1)S(1)}, u32[]{:S(2)}, u32[]{:S(2)}) async-start(bf16[16,10,2048]{2,1,0:T(8,128)(2,1)} %reshape.112), calls=%async_computation | async-start | bytes 2097152 | tf_op jit(solution)/shard_map/while/body/eval_jaxpr/all_to_all | solution.py:75
  69.6 21.1 %all-to-all-start.1 = ((bf16[2,80,2048]{2,0,1:T(2,128)(2,1)}), bf16[2,80,2048]{2,0,1:T(2,128)(2,1)S(1)}, u32[]{:S(2)}, u32[]{:S(2)}) async-start(bf16[2,80,2048]{2,0,1:T(2,128)(2,1)} %copy.142), calls=%async_computation.1 | async-start | bytes 1310720 | tf_op jit(solution)/shard_map/while/body/eval_jaxpr/all_to_all | solution.py:79
  99.6 29.6 %all-to-all-start = ((bf16[16,10,2048]{2,1,0:T(8,128)(2,1)}), bf16[16,10,2048]{2,1,0:T(8,128)(2,1)S(1)}, u32[]{:S(2)}, u32[]{:S(2)}) async-start(bf16[16,10,2048]{2,1,0:T(8,128)(2,1)} %reshape.112), calls=%async_computation | async-start | bytes 2097152 | tf_op jit(solution)/shard_map/while/body/eval_jaxpr/all_to_all | solution.py:75
  140.1 21.1 %all-to-all-start.1 = ((bf16[2,80,2048]{2,0,1:T(2,128)(2,1)}), bf16[2,80,2048]{2,0,1:T(2,128)(2,1)S(1)}, u32[]{:S(2)}, u32[]{:S(2)}) async-start(bf16[2,80,2048]{2,0,1:T(2,128)(2,1)} %copy.142), calls=%async_computation.1 | async-start | bytes 1310720 | tf_op jit(solution)/shard_map/while/body/eval_jaxpr/all_to_all | solution.py:79
  172.3 29.3 %all-to-all-start = ((bf16[16,10,2048]{2,1,0:T(8,128)(2,1)}), bf16[16,10,2048]{2,1,0:T(8,128)(2,1)S(1)}, u32[]{:S(2)}, u32[]{:S(2)}) async-start(bf16[16,10,2048]{2,1,0:T(8,128)(2,1)} %reshape.112), calls=%async_computation | async-start | bytes 2097152 | tf_op jit(solution)/shard_map/while/body/eval_jaxpr/all_to_all | solution.py:75
  244.5 29.3 %all-to-all-start = ((bf16[16,10,2048]{2,1,0:T(8,128)(2,1)}), bf16[16,10,2048]{2,1,0:T(8,128)(2,1)S(1)}, u32[]{:S(2)}, u32[]{:S(2)}) async-start(bf16[16,10,2048]{2,1,0:T(8,128)(2,1)} %reshape.112), calls=%async_computation | async-start | bytes 2097152 | tf_op jit(solution)/shard_map/while/body/eval_jaxpr/all_to_all | solution.py:75
  316.6 29.3 %all-to-all-start = ((bf16[16,10,2048]{2,1,0:T(8,128)(2,1)}), bf16[16,10,2048]{2,1,0:T(8,128)(2,1)S(1)}, u32[]{:S(2)}, u32[]{:S(2)}) async-start(bf16[16,10,2048]{2,1,0:T(8,128)(2,1)} %reshape.112), calls=%async_computation | async-start | bytes 2097152 | tf_op jit(solution)/shard_map/while/body/eval_jaxpr/all_to_all | solution.py:75
  388.7 29.3 %all-to-all-start = ((bf16[16,10,2048]{2,1,0:T(8,128)(2,1)}), bf16[16,10,2048]{2,1,0:T(8,128)(2,1)S(1)}, u32[]{:S(2)}, u32[]{:S(2)}) async-start(bf16[16,10,2048]{2,1,0:T(8,128)(2,1)} %reshape.112), calls=%async_computation | async-start | bytes 2097152 | tf_op jit(solution)/shard_map/while/body/eval_jaxpr/all_to_all | solution.py:75
  428.9 21.0 %all-to-all-start.1 = ((bf16[2,80,2048]{2,0,1:T(2,128)(2,1)}), bf16[2,80,2048]{2,0,1:T(2,128)(2,1)S(1)}, u32[]{:S(2)}, u32[]{:S(2)}) async-start(bf16[2,80,2048]{2,0,1:T(2,128)(2,1)} %copy.142), calls=%async_computation.1 | async-start | bytes 1310720 | tf_op jit(solution)/shard_map/while/body/eval_jaxpr/all_to_all | solution.py:79
  460.9 29.3 %all-to-all-start = ((bf16[16,10,2048]{2,1,0:T(8,128)(2,1)}), bf16[16,10,2048]{2,1,0:T(8,128)(2,1)S(1)}, u32[]{:S(2)}, u32[]{:S(2)}) async-start(bf16[16,10,2048]{2,1,0:T(8,128)(2,1)} %reshape.112), calls=%async_computation | async-start | bytes 2097152 | tf_op jit(solution)/shard_map/while/body/eval_jaxpr/all_to_all | solution.py:75
  533.0 29.3 %all-to-all-start = ((bf16[16,10,2048]{2,1,0:T(8,128)(2,1)}), bf16[16,10,2048]{2,1,0:T(8,128)(2,1)S(1)}, u32[]{:S(2)}, u32[]{:S(2)}) async-start(bf16[16,10,2048]{2,1,0:T(8,128)(2,1)} %reshape.112), calls=%async_computation | async-start | bytes 2097152 | tf_op jit(solution)/shard_map/while/body/eval_jaxpr/all_to_all | solution.py:75
  605.2 29.3 %all-to-all-start = ((bf16[16,10,2048]{2,1,0:T(8,128)(2,1)}), bf16[16,10,2048]{2,1,0:T(8,128)(2,1)S(1)}, u32[]{:S(2)}, u32[]{:S(2)}) async-start(bf16[16,10,2048]{2,1,0:T(8,128)(2,1)} %reshape.112), calls=%async_computation | async-start | bytes 2097152 | tf_op jit(solution)/shard_map/while/body/eval_jaxpr/all_to_all | solution.py:75
  680.9 29.0 %all-to-all-start.2 = ((bf16[16,10,2048]{2,1,0:T(8,128)(2,1)}), bf16[16,10,2048]{2,1,0:T(8,128)(2,1)S(1)}, u32[]{:S(2)}, u32[]{:S(2)}) async-start(bf16[16,10,2048]{2,1,0:T(8,128)(2,1)} %reshape.114), calls=%async_computation.2 | async-start | bytes 2097152 | tf_op jit(solution)/shard_map/while/body/eval_jaxpr/all_to_all | solution.py:75
  753.6 29.2 %all-to-all-start.2 = ((bf16[16,10,2048]{2,1,0:T(8,128)(2,1)}), bf16[16,10,2048]{2,1,0:T(8,128)(2,1)S(1)}, u32[]{:S(2)}, u32[]{:S(2)}) async-start(bf16[16,10,2048]{2,1,0:T(8,128)(2,1)} %reshape.114), calls=%async_computation.2 | async-start | bytes 2097152 | tf_op jit(solution)/shard_map/while/body/eval_jaxpr/all_to_all | solution.py:75
  827.3 28.7 %all-to-all-start.2 = ((bf16[16,10,2048]{2,1,0:T(8,128)(2,1)}), bf16[16,10,2048]{2,1,0:T(8,128)(2,1)S(1)}, u32[]{:S(2)}, u32[]{:S(2)}) async-start(bf16[16,10,2048]{2,1,0:T(8,128)(2,1)} %reshape.114), calls=%async_computation.2 | async-start | bytes 2097152 | tf_op jit(solution)/shard_map/while/body/eval_jaxpr/all_to_all | solution.py:75
  900.3 28.7 %all-to-all-start.2 = ((bf16[16,10,2048]{2,1,0:T(8,128)(2,1)}), bf16[16,10,2048]{2,1,0:T(8,128)(2,1)S(1)}, u32[]{:S(2)}, u32[]{:S(2)}) async-start(bf16[16,10,2048]{2,1,0:T(8,128)(2,1)} %reshape.114), calls=%async_computation.2 | async-start | bytes 2097152 | tf_op jit(solution)/shard_map/while/body/eval_jaxpr/all_to_all | solution.py:75
  973.3 28.7 %all-to-all-start.2 = ((bf16[16,10,2048]{2,1,0:T(8,128)(2,1)}), bf16[16,10,2048]{2,1,0:T(8,128)(2,1)S(1)}, u32[]{:S(2)}, u32[]{:S(2)}) async-start(bf16[16,10,2048]{2,1,0:T(8,128)(2,1)} %reshape.114), calls=%async_computation.2 | async-start | bytes 2097152 | tf_op jit(solution)/shard_map/while/body/eval_jaxpr/all_to_all | solution.py:75
  1046.4 28.7 %all-to-all-start.2 = ((bf16[16,10,2048]{2,1,0:T(8,128)(2,1)}), bf16[16,10,2048]{2,1,0:T(8,128)(2,1)S(1)}, u32[]{:S(2)}, u32[]{:S(2)}) async-start(bf16[16,10,2048]{2,1,0:T(8,128)(2,1)} %reshape.114), calls=%async_computation.2 | async-start | bytes 2097152 | tf_op jit(solution)/shard_map/while/body/eval_jaxpr/all_to_all | solution.py:75
  1119.4 28.7 %all-to-all-start.2 = ((bf16[16,10,2048]{2,1,0:T(8,128)(2,1)}), bf16[16,10,2048]{2,1,0:T(8,128)(2,1)S(1)}, u32[]{:S(2)}, u32[]{:S(2)}) async-start(bf16[16,10,2048]{2,1,0:T(8,128)(2,1)} %reshape.114), calls=%async_computation.2 | async-start | bytes 2097152 | tf_op jit(solution)/shard_map/while/body/eval_jaxpr/all_to_all | solution.py:75
  1192.4 28.7 %all-to-all-start.2 = ((bf16[16,10,2048]{2,1,0:T(8,128)(2,1)}), bf16[16,10,2048]{2,1,0:T(8,128)(2,1)S(1)}, u32[]{:S(2)}, u32[]{:S(2)}) async-start(bf16[16,10,2048]{2,1,0:T(8,128)(2,1)} %reshape.114), calls=%async_computation.2 | async-start | bytes 2097152 | tf_op jit(solution)/shard_map/while/body/eval_jaxpr/all_to_all | solution.py:75
  1265.5 28.7 %all-to-all-start.2 = ((bf16[16,10,2048]{2,1,0:T(8,128)(2,1)}), bf16[16,10,2048]{2,1,0:T(8,128)(2,1)S(1)}, u32[]{:S(2)}, u32[]{:S(2)}) async-start(bf16[16,10,2048]{2,1,0:T(8,128)(2,1)} %reshape.114), calls=%async_computation.2 | async-start | bytes 2097152 | tf_op jit(solution)/shard_map/while/body/eval_jaxpr/all_to_all | solution.py:75
  1344.7 26.6 %reduce-scatter.4.cloned.1.call-start = ((), (), s32[]{:S(2)}) async-start(), calls=%async_computation.7 | async-start | bytes 6291456 | tf_op jit(solution)/shard_map/reduce_scatter | solution.py:228
  1354.4 33.0 %reduce-scatter.8.cloned.1.call-start = ((), (), s32[]{:S(2)}) async-start(), calls=%async_computation.9 | async-start | bytes 6291456 | tf_op jit(solution)/shard_map/reduce_scatter | solution.py:234
  (69 other events, 552.8 us)
Sparse Core Ops, SparseCore 0:
  1344.8 10.1 reduce-scatter.5
  1357.9 13.3 reduce-scatter.3
  1374.1 13.3 reduce-scatter.7
where the time goes:
time: 1400 us; the launch traced here: 1390 us
  waiting for transfers between devices  712 us (51%)
  local copies, waits for them, and re-layouts  208 us (15%)
  matrix products  195 us (14%)
  starting transfers between devices  179 us (13%)
  other arithmetic  83.9 us (6%)
    all_to_all x18, waiting for transfers between devices, send_out(): lax.all_to_all(buffer, 'expert', split_axis=0, concat_axis=1, tiled=True)  421 us
    all_to_all x18, waiting for transfers between devices, send_back(): lax.all_to_all(buffer, 'expert', split_axis=1, concat_axis=0, tiled=True)  231 us
    dynamic_slice x81, local copies, waits for them, and re-layouts, keep_slice(): previous = lax.dynamic_index_in_dim(stored, at_index, 0, keepdims=False)  70.5 us
    all_to_all x18, starting transfers between devices, send_out(): lax.all_to_all(buffer, 'expert', split_axis=0, concat_axis=1, tiled=True)  69.2 us
    all_to_all x18, starting transfers between devices, send_back(): lax.all_to_all(buffer, 'expert', split_axis=1, concat_axis=0, tiled=True)  64.1 us
    dynamic_update_slice x36, other arithmetic, keep_slice(): lax.dynamic_update_index_in_dim(stored, jnp.where(is_valid, new_value, pr...  55.1 us
    ppermute x18, starting transfers between devices, from_behind(): return lax.ppermute(block, axis, route)  46.1 us
    dot_general x8, matrix products, expert_backward(): jnp.einsum('erx,efx->erf', out_grad, down_w, preferred_element_type=jnp.f...  38.1 us
  transfers between devices with their start and end apart: 57, of which 48 were waited for; matrix products, arithmetic and copies ran while one was open for 12% of the time, Pallas kernels for 0%

commit v1 on v0

--- a/solution.py
+++ b/solution.py
@@ -4,6 +4,12 @@
 from jax.sharding import PartitionSpec as P
 
 epsilon = 1e-06
+
+
+def trade_parts(x, mesh_axis, split, join):
+    parts = jnp.split(x, lax.axis_size(mesh_axis), axis=split)
+    incoming = lax.all_to_all(jnp.stack(parts), mesh_axis, 0, 0)
+    return jnp.concatenate(incoming, axis=join)
 
 
 def from_behind(block, axis, distance):
@@ -76,7 +82,7 @@
 
 
 def send_back(buffer):
-    return lax.all_to_all(buffer, "expert", split_axis=1, concat_axis=0, tiled=True)
+    return trade_parts(buffer, "expert", 1, 0)
 
 
 def on_device(tokens_in, cotangent, routes, router_weights, norm_gain, w_gate, w_up, w_down):

time: 1400 us -> 1500 us (1.071)
  local copies, waits for them, and re-layouts: 208 us -> 312 us
  matrix products: 195 us -> 179 us
    while x0 -> x126, local copies, waits for them, and re-layouts: none -> 87.2 us
    another operation x33 -> x81, local copies, waits for them, and re-layouts: 24.9 us -> 39.9 us
  transfers between devices with their start and end apart: 57 -> 57, of which waited for: 48 -> 48; matrix products, arithmetic and copies ran while one was open for 12% -> 11% of each run, Pallas kernels for 0% -> 0%
where the time goes in v1:
time: 1500 us; the launch traced here: 1480 us
  waiting for transfers between devices  712 us (47%)
  local copies, waits for them, and re-layouts  312 us (21%)
  starting transfers between devices  181 us (12%)
  matrix products  179 us (12%)
  other arithmetic  81.8 us (5%)
    all_to_all x18, waiting for transfers between devices, send_out(): lax.all_to_all(buffer, 'expert', split_axis=0, concat_axis=1, tiled=True)  413 us
    all_to_all x18, waiting for transfers between devices, trade_parts(): incoming = lax.all_to_all(jnp.stack(parts), mesh_axis, 0, 0)  231 us
    while x126, local copies, waits for them, and re-layouts  87.2 us
    dynamic_slice x81, local copies, waits for them, and re-layouts, keep_slice(): previous = lax.dynamic_index_in_dim(stored, at_index, 0, keepdims=False)  78 us
    all_to_all x18, starting transfers between devices, send_out(): lax.all_to_all(buffer, 'expert', split_axis=0, concat_axis=1, tiled=True)  69.2 us
    all_to_all x18, starting transfers between devices, trade_parts(): incoming = lax.all_to_all(jnp.stack(parts), mesh_axis, 0, 0)  64.1 us
    dynamic_update_slice x36, other arithmetic, keep_slice(): lax.dynamic_update_index_in_dim(stored, jnp.where(is_valid, new_value, pr...  51.7 us
    ppermute x18, starting transfers between devices, from_behind(): return lax.ppermute(block, axis, route)  47.8 us
  transfers between devices with their start and end apart: 57, of which 48 were waited for; matrix products, arithmetic and copies ran while one was open for 11% of the time, Pallas kernels for 0%

profile of v1, /device:TPU:0, one launch (start us, length us, event | category | flops | bytes accessed | tf_op | source)
XLA Modules:
  0.0 1484.4 jit_solution(9513337331960689952)
XLA Ops:
  22.9 705.2 %while.47 = (s32[]{:T(128)}, bf16[16,2048]{1,0:T(8,128)(2,1)S(1)}, bf16[8,16,2048]{2,1,0:T(8,128)(2,1)}, bf16[8,2,80,2048]{3,2,0,1:T(8,128)(2,1)}, f32[8,2,80,51...) while((s32[]{:T(128)}, bf16[16,2048]{1,0:T(8,128)(2,1)S(1)}, ...), condition=%wide.region_8.9_spmd, body=%wide.region_4.0_spmd.sunk | while | flops 1082097664 | bytes 79006560 | solution.py:158
  36.9 23.8 %all-to-all-done = bf16[16,10,2048]{2,1,0:T(8,128)(2,1)S(1)} async-done(((bf16[16,10,2048]{2,1,0:T(8,128)(2,1)}), bf16[16,10,2048]{2,1,0:T(8,128)(2,1)S(1)}, u32[]{:S(2)}, u32[]{:S(2)}) %all-to-all-start) | async-done | bytes 655392 | tf_op jit(solution)/shard_map/while/body/eval_jaxpr/all_to_all | solution.py:81
  113.0 24.0 %all-to-all-done = bf16[16,10,2048]{2,1,0:T(8,128)(2,1)S(1)} async-done(((bf16[16,10,2048]{2,1,0:T(8,128)(2,1)}), bf16[16,10,2048]{2,1,0:T(8,128)(2,1)S(1)}, u32[]{:S(2)}, u32[]{:S(2)}) %all-to-all-start) | async-done | bytes 655392 | tf_op jit(solution)/shard_map/while/body/eval_jaxpr/all_to_all | solution.py:81
  191.7 23.7 %all-to-all-done = bf16[16,10,2048]{2,1,0:T(8,128)(2,1)S(1)} async-done(((bf16[16,10,2048]{2,1,0:T(8,128)(2,1)}), bf16[16,10,2048]{2,1,0:T(8,128)(2,1)S(1)}, u32[]{:S(2)}, u32[]{:S(2)}) %all-to-all-start) | async-done | bytes 655392 | tf_op jit(solution)/shard_map/while/body/eval_jaxpr/all_to_all | solution.py:81
  269.9 23.7 %all-to-all-done = bf16[16,10,2048]{2,1,0:T(8,128)(2,1)S(1)} async-done(((bf16[16,10,2048]{2,1,0:T(8,128)(2,1)}), bf16[16,10,2048]{2,1,0:T(8,128)(2,1)S(1)}, u32[]{:S(2)}, u32[]{:S(2)}) %all-to-all-start) | async-done | bytes 655392 | tf_op jit(solution)/shard_map/while/body/eval_jaxpr/all_to_all | solution.py:81
  347.9 23.7 %all-to-all-done = bf16[16,10,2048]{2,1,0:T(8,128)(2,1)S(1)} async-done(((bf16[16,10,2048]{2,1,0:T(8,128)(2,1)}), bf16[16,10,2048]{2,1,0:T(8,128)(2,1)S(1)}, u32[]{:S(2)}, u32[]{:S(2)}) %all-to-all-start) | async-done | bytes 655392 | tf_op jit(solution)/shard_map/while/body/eval_jaxpr/all_to_all | solution.py:81
  395.3 12.9 all-to-all-done.1
  426.1 23.7 %all-to-all-done = bf16[16,10,2048]{2,1,0:T(8,128)(2,1)S(1)} async-done(((bf16[16,10,2048]{2,1,0:T(8,128)(2,1)}), bf16[16,10,2048]{2,1,0:T(8,128)(2,1)S(1)}, u32[]{:S(2)}, u32[]{:S(2)}) %all-to-all-start) | async-done | bytes 655392 | tf_op jit(solution)/shard_map/while/body/eval_jaxpr/all_to_all | solution.py:81
  504.1 23.7 %all-to-all-done = bf16[16,10,2048]{2,1,0:T(8,128)(2,1)S(1)} async-done(((bf16[16,10,2048]{2,1,0:T(8,128)(2,1)}), bf16[16,10,2048]{2,1,0:T(8,128)(2,1)S(1)}, u32[]{:S(2)}, u32[]{:S(2)}) %all-to-all-start) | async-done | bytes 655392 | tf_op jit(solution)/shard_map/while/body/eval_jaxpr/all_to_all | solution.py:81
  582.2 23.7 %all-to-all-done = bf16[16,10,2048]{2,1,0:T(8,128)(2,1)S(1)} async-done(((bf16[16,10,2048]{2,1,0:T(8,128)(2,1)}), bf16[16,10,2048]{2,1,0:T(8,128)(2,1)S(1)}, u32[]{:S(2)}, u32[]{:S(2)}) %all-to-all-start) | async-done | bytes 655392 | tf_op jit(solution)/shard_map/while/body/eval_jaxpr/all_to_all | solution.py:81
  629.6 12.9 all-to-all-done.1
  660.4 23.7 %all-to-all-done = bf16[16,10,2048]{2,1,0:T(8,128)(2,1)S(1)} async-done(((bf16[16,10,2048]{2,1,0:T(8,128)(2,1)}), bf16[16,10,2048]{2,1,0:T(8,128)(2,1)S(1)}, u32[]{:S(2)}, u32[]{:S(2)}) %all-to-all-start) | async-done | bytes 655392 | tf_op jit(solution)/shard_map/while/body/eval_jaxpr/all_to_all | solution.py:81
  699.7 12.9 all-to-all-done.1
  734.3 692.4 %while.48 = (s32[]{:T(128)}, bf16[16,2048]{1,0:T(8,128)(2,1)S(1)}, bf16[8,2,80,2048]{3,2,1,0:T(8,128)(2,1)}, bf16[8,2,80,512]{3,2,0,1:T(8,128)(2,1)}, bf16[8,2,8...) while((s32[]{:T(128)}, bf16[16,2048]{1,0:T(8,128)(2,1)S(1)}, ...), condition=%wide.region_15.16_spmd, body=%wide.region_10.15_spmd.sunk | while | flops 1031094272 | bytes 79396456 | solution.py:220
  743.3 22.4 %all-to-all-done.2 = bf16[16,10,2048]{2,1,0:T(8,128)(2,1)S(1)} async-done(((bf16[16,10,2048]{2,1,0:T(8,128)(2,1)}), bf16[16,10,2048]{2,1,0:T(8,128)(2,1)S(1)}, u32[]{:S(2)}, u32[]{:S(2)}) %all-to-all-start.2) | async-done | bytes 655392 | tf_op jit(solution)/shard_map/while/body/eval_jaxpr/all_to_all | solution.py:81
  819.9 22.6 %all-to-all-done.2 = bf16[16,10,2048]{2,1,0:T(8,128)(2,1)S(1)} async-done(((bf16[16,10,2048]{2,1,0:T(8,128)(2,1)}), bf16[16,10,2048]{2,1,0:T(8,128)(2,1)S(1)}, u32[]{:S(2)}, u32[]{:S(2)}) %all-to-all-start.2) | async-done | bytes 655392 | tf_op jit(solution)/shard_map/while/body/eval_jaxpr/all_to_all | solution.py:81
  897.4 22.1 %all-to-all-done.2 = bf16[16,10,2048]{2,1,0:T(8,128)(2,1)S(1)} async-done(((bf16[16,10,2048]{2,1,0:T(8,128)(2,1)}), bf16[16,10,2048]{2,1,0:T(8,128)(2,1)S(1)}, u32[]{:S(2)}, u32[]{:S(2)}) %all-to-all-start.2) | async-done | bytes 655392 | tf_op jit(solution)/shard_map/while/body/eval_jaxpr/all_to_all | solution.py:81
  974.3 22.1 %all-to-all-done.2 = bf16[16,10,2048]{2,1,0:T(8,128)(2,1)S(1)} async-done(((bf16[16,10,2048]{2,1,0:T(8,128)(2,1)}), bf16[16,10,2048]{2,1,0:T(8,128)(2,1)S(1)}, u32[]{:S(2)}, u32[]{:S(2)}) %all-to-all-start.2) | async-done | bytes 655392 | tf_op jit(solution)/shard_map/while/body/eval_jaxpr/all_to_all | solution.py:81
  1051.2 22.1 %all-to-all-done.2 = bf16[16,10,2048]{2,1,0:T(8,128)(2,1)S(1)} async-done(((bf16[16,10,2048]{2,1,0:T(8,128)(2,1)}), bf16[16,10,2048]{2,1,0:T(8,128)(2,1)S(1)}, u32[]{:S(2)}, u32[]{:S(2)}) %all-to-all-start.2) | async-done | bytes 655392 | tf_op jit(solution)/shard_map/while/body/eval_jaxpr/all_to_all | solution.py:81
  1128.1 22.1 %all-to-all-done.2 = bf16[16,10,2048]{2,1,0:T(8,128)(2,1)S(1)} async-done(((bf16[16,10,2048]{2,1,0:T(8,128)(2,1)}), bf16[16,10,2048]{2,1,0:T(8,128)(2,1)S(1)}, u32[]{:S(2)}, u32[]{:S(2)}) %all-to-all-start.2) | async-done | bytes 655392 | tf_op jit(solution)/shard_map/while/body/eval_jaxpr/all_to_all | solution.py:81
  1205.0 22.1 %all-to-all-done.2 = bf16[16,10,2048]{2,1,0:T(8,128)(2,1)S(1)} async-done(((bf16[16,10,2048]{2,1,0:T(8,128)(2,1)}), bf16[16,10,2048]{2,1,0:T(8,128)(2,1)S(1)}, u32[]{:S(2)}, u32[]{:S(2)}) %all-to-all-start.2) | async-done | bytes 655392 | tf_op jit(solution)/shard_map/while/body/eval_jaxpr/all_to_all | solution.py:81
  1281.9 22.1 %all-to-all-done.2 = bf16[16,10,2048]{2,1,0:T(8,128)(2,1)S(1)} async-done(((bf16[16,10,2048]{2,1,0:T(8,128)(2,1)}), bf16[16,10,2048]{2,1,0:T(8,128)(2,1)S(1)}, u32[]{:S(2)}, u32[]{:S(2)}) %all-to-all-start.2) | async-done | bytes 655392 | tf_op jit(solution)/shard_map/while/body/eval_jaxpr/all_to_all | solution.py:81
  1358.8 22.1 %all-to-all-done.2 = bf16[16,10,2048]{2,1,0:T(8,128)(2,1)S(1)} async-done(((bf16[16,10,2048]{2,1,0:T(8,128)(2,1)}), bf16[16,10,2048]{2,1,0:T(8,128)(2,1)S(1)}, u32[]{:S(2)}, u32[]{:S(2)}) %all-to-all-start.2) | async-done | bytes 655392 | tf_op jit(solution)/shard_map/while/body/eval_jaxpr/all_to_all | solution.py:81
  1461.6 16.2 %reduce-scatter.8.cloned.1.call-done = bf16[2,256,2048]{2,1,0:T(8,128)(2,1)} async-done(((bf16[2,512,2048]{2,1,0:T(8,128)(2,1)}), bf16[2,256,2048]{2,1,0:T(8,128)(2,1)}) %reduce-scatter.8.cloned.1.call-update) | async-done | bytes 2097168 | tf_op jit(solution)/shard_map/reduce_scatter | solution.py:240
  (1007 shorter events, 1148.4 us)
Async XLA Ops:
  7.2 1448.2 %reduce-scatter.6.cloned.1.call-start = ((), (), s32[]{:S(2)}) async-start(), calls=%async_computation.8 | async-start | bytes 6291456 | tf_op jit(solution)/shard_map/reduce_scatter | solution.py:237
  27.6 33.0 %all-to-all-start = ((bf16[16,10,2048]{2,1,0:T(8,128)(2,1)}), bf16[16,10,2048]{2,1,0:T(8,128)(2,1)S(1)}, u32[]{:S(2)}, u32[]{:S(2)}) async-start(bf16[16,10,2048]{2,1,0:T(8,128)(2,1)} %reshape.110), calls=%async_computation | async-start | bytes 2097152 | tf_op jit(solution)/shard_map/while/body/eval_jaxpr/all_to_all | solution.py:81
  76.2 21.1 %all-to-all-start.1 = ((bf16[8,2,10,2048]{3,1,2,0:T(2,128)(2,1)}), bf16[8,2,10,2048]{3,1,2,0:T(2,128)(2,1)S(1)}, u32[]{:S(2)}, u32[]{:S(2)}) async-start(bf16[8,2,10,2048]{3,1,2,0:T(2,128)(2,1)} %constant_dynamic-update-slice_fusion.39), calls=%async_computation.1 | async-start | bytes 1310720 | tf_op jit(solution)/shard_map/while/body/eval_jaxpr/all_to_all | solution.py:11
  107.4 29.6 %all-to-all-start = ((bf16[16,10,2048]{2,1,0:T(8,128)(2,1)}), bf16[16,10,2048]{2,1,0:T(8,128)(2,1)S(1)}, u32[]{:S(2)}, u32[]{:S(2)}) async-start(bf16[16,10,2048]{2,1,0:T(8,128)(2,1)} %reshape.110), calls=%async_computation | async-start | bytes 2097152 | tf_op jit(solution)/shard_map/while/body/eval_jaxpr/all_to_all | solution.py:81
  152.5 21.1 %all-to-all-start.1 = ((bf16[8,2,10,2048]{3,1,2,0:T(2,128)(2,1)}), bf16[8,2,10,2048]{3,1,2,0:T(2,128)(2,1)S(1)}, u32[]{:S(2)}, u32[]{:S(2)}) async-start(bf16[8,2,10,2048]{3,1,2,0:T(2,128)(2,1)} %constant_dynamic-update-slice_fusion.39), calls=%async_computation.1 | async-start | bytes 1310720 | tf_op jit(solution)/shard_map/while/body/eval_jaxpr/all_to_all | solution.py:11
  186.1 29.3 %all-to-all-start = ((bf16[16,10,2048]{2,1,0:T(8,128)(2,1)}), bf16[16,10,2048]{2,1,0:T(8,128)(2,1)S(1)}, u32[]{:S(2)}, u32[]{:S(2)}) async-start(bf16[16,10,2048]{2,1,0:T(8,128)(2,1)} %reshape.110), calls=%async_computation | async-start | bytes 2097152 | tf_op jit(solution)/shard_map/while/body/eval_jaxpr/all_to_all | solution.py:81
  264.2 29.3 %all-to-all-start = ((bf16[16,10,2048]{2,1,0:T(8,128)(2,1)}), bf16[16,10,2048]{2,1,0:T(8,128)(2,1)S(1)}, u32[]{:S(2)}, u32[]{:S(2)}) async-start(bf16[16,10,2048]{2,1,0:T(8,128)(2,1)} %reshape.110), calls=%async_computation | async-start | bytes 2097152 | tf_op jit(solution)/shard_map/while/body/eval_jaxpr/all_to_all | solution.py:81
  342.3 29.3 %all-to-all-start = ((bf16[16,10,2048]{2,1,0:T(8,128)(2,1)}), bf16[16,10,2048]{2,1,0:T(8,128)(2,1)S(1)}, u32[]{:S(2)}, u32[]{:S(2)}) async-start(bf16[16,10,2048]{2,1,0:T(8,128)(2,1)} %reshape.110), calls=%async_computation | async-start | bytes 2097152 | tf_op jit(solution)/shard_map/while/body/eval_jaxpr/all_to_all | solution.py:81
  420.4 29.3 %all-to-all-start = ((bf16[16,10,2048]{2,1,0:T(8,128)(2,1)}), bf16[16,10,2048]{2,1,0:T(8,128)(2,1)S(1)}, u32[]{:S(2)}, u32[]{:S(2)}) async-start(bf16[16,10,2048]{2,1,0:T(8,128)(2,1)} %reshape.110), calls=%async_computation | async-start | bytes 2097152 | tf_op jit(solution)/shard_map/while/body/eval_jaxpr/all_to_all | solution.py:81
  465.2 21.0 %all-to-all-start.1 = ((bf16[8,2,10,2048]{3,1,2,0:T(2,128)(2,1)}), bf16[8,2,10,2048]{3,1,2,0:T(2,128)(2,1)S(1)}, u32[]{:S(2)}, u32[]{:S(2)}) async-start(bf16[8,2,10,2048]{3,1,2,0:T(2,128)(2,1)} %constant_dynamic-update-slice_fusion.39), calls=%async_computation.1 | async-start | bytes 1310720 | tf_op jit(solution)/shard_map/while/body/eval_jaxpr/all_to_all | solution.py:11
  498.5 29.3 %all-to-all-start = ((bf16[16,10,2048]{2,1,0:T(8,128)(2,1)}), bf16[16,10,2048]{2,1,0:T(8,128)(2,1)S(1)}, u32[]{:S(2)}, u32[]{:S(2)}) async-start(bf16[16,10,2048]{2,1,0:T(8,128)(2,1)} %reshape.110), calls=%async_computation | async-start | bytes 2097152 | tf_op jit(solution)/shard_map/while/body/eval_jaxpr/all_to_all | solution.py:81
  576.6 29.3 %all-to-all-start = ((bf16[16,10,2048]{2,1,0:T(8,128)(2,1)}), bf16[16,10,2048]{2,1,0:T(8,128)(2,1)S(1)}, u32[]{:S(2)}, u32[]{:S(2)}) async-start(bf16[16,10,2048]{2,1,0:T(8,128)(2,1)} %reshape.110), calls=%async_computation | async-start | bytes 2097152 | tf_op jit(solution)/shard_map/while/body/eval_jaxpr/all_to_all | solution.py:81
  654.8 29.3 %all-to-all-start = ((bf16[16,10,2048]{2,1,0:T(8,128)(2,1)}), bf16[16,10,2048]{2,1,0:T(8,128)(2,1)S(1)}, u32[]{:S(2)}, u32[]{:S(2)}) async-start(bf16[16,10,2048]{2,1,0:T(8,128)(2,1)} %reshape.110), calls=%async_computation | async-start | bytes 2097152 | tf_op jit(solution)/shard_map/while/body/eval_jaxpr/all_to_all | solution.py:81
  736.7 29.0 %all-to-all-start.2 = ((bf16[16,10,2048]{2,1,0:T(8,128)(2,1)}), bf16[16,10,2048]{2,1,0:T(8,128)(2,1)S(1)}, u32[]{:S(2)}, u32[]{:S(2)}) async-start(bf16[16,10,2048]{2,1,0:T(8,128)(2,1)} %reshape.112), calls=%async_computation.2 | async-start | bytes 2097152 | tf_op jit(solution)/shard_map/while/body/eval_jaxpr/all_to_all | solution.py:81
  813.3 29.2 %all-to-all-start.2 = ((bf16[16,10,2048]{2,1,0:T(8,128)(2,1)}), bf16[16,10,2048]{2,1,0:T(8,128)(2,1)S(1)}, u32[]{:S(2)}, u32[]{:S(2)}) async-start(bf16[16,10,2048]{2,1,0:T(8,128)(2,1)} %reshape.112), calls=%async_computation.2 | async-start | bytes 2097152 | tf_op jit(solution)/shard_map/while/body/eval_jaxpr/all_to_all | solution.py:81
  890.8 28.7 %all-to-all-start.2 = ((bf16[16,10,2048]{2,1,0:T(8,128)(2,1)}), bf16[16,10,2048]{2,1,0:T(8,128)(2,1)S(1)}, u32[]{:S(2)}, u32[]{:S(2)}) async-start(bf16[16,10,2048]{2,1,0:T(8,128)(2,1)} %reshape.112), calls=%async_computation.2 | async-start | bytes 2097152 | tf_op jit(solution)/shard_map/while/body/eval_jaxpr/all_to_all | solution.py:81
  967.7 28.7 %all-to-all-start.2 = ((bf16[16,10,2048]{2,1,0:T(8,128)(2,1)}), bf16[16,10,2048]{2,1,0:T(8,128)(2,1)S(1)}, u32[]{:S(2)}, u32[]{:S(2)}) async-start(bf16[16,10,2048]{2,1,0:T(8,128)(2,1)} %reshape.112), calls=%async_computation.2 | async-start | bytes 2097152 | tf_op jit(solution)/shard_map/while/body/eval_jaxpr/all_to_all | solution.py:81
  1044.6 28.7 %all-to-all-start.2 = ((bf16[16,10,2048]{2,1,0:T(8,128)(2,1)}), bf16[16,10,2048]{2,1,0:T(8,128)(2,1)S(1)}, u32[]{:S(2)}, u32[]{:S(2)}) async-start(bf16[16,10,2048]{2,1,0:T(8,128)(2,1)} %reshape.112), calls=%async_computation.2 | async-start | bytes 2097152 | tf_op jit(solution)/shard_map/while/body/eval_jaxpr/all_to_all | solution.py:81
  1121.5 28.7 %all-to-all-start.2 = ((bf16[16,10,2048]{2,1,0:T(8,128)(2,1)}), bf16[16,10,2048]{2,1,0:T(8,128)(2,1)S(1)}, u32[]{:S(2)}, u32[]{:S(2)}) async-start(bf16[16,10,2048]{2,1,0:T(8,128)(2,1)} %reshape.112), calls=%async_computation.2 | async-start | bytes 2097152 | tf_op jit(solution)/shard_map/while/body/eval_jaxpr/all_to_all | solution.py:81
  1198.4 28.7 %all-to-all-start.2 = ((bf16[16,10,2048]{2,1,0:T(8,128)(2,1)}), bf16[16,10,2048]{2,1,0:T(8,128)(2,1)S(1)}, u32[]{:S(2)}, u32[]{:S(2)}) async-start(bf16[16,10,2048]{2,1,0:T(8,128)(2,1)} %reshape.112), calls=%async_computation.2 | async-start | bytes 2097152 | tf_op jit(solution)/shard_map/while/body/eval_jaxpr/all_to_all | solution.py:81
  1275.3 28.7 %all-to-all-start.2 = ((bf16[16,10,2048]{2,1,0:T(8,128)(2,1)}), bf16[16,10,2048]{2,1,0:T(8,128)(2,1)S(1)}, u32[]{:S(2)}, u32[]{:S(2)}) async-start(bf16[16,10,2048]{2,1,0:T(8,128)(2,1)} %reshape.112), calls=%async_computation.2 | async-start | bytes 2097152 | tf_op jit(solution)/shard_map/while/body/eval_jaxpr/all_to_all | solution.py:81
  1352.2 28.7 %all-to-all-start.2 = ((bf16[16,10,2048]{2,1,0:T(8,128)(2,1)}), bf16[16,10,2048]{2,1,0:T(8,128)(2,1)S(1)}, u32[]{:S(2)}, u32[]{:S(2)}) async-start(bf16[16,10,2048]{2,1,0:T(8,128)(2,1)} %reshape.112), calls=%async_computation.2 | async-start | bytes 2097152 | tf_op jit(solution)/shard_map/while/body/eval_jaxpr/all_to_all | solution.py:81
  1435.0 26.6 %reduce-scatter.4.cloned.1.call-start = ((), (), s32[]{:S(2)}) async-start(), calls=%async_computation.7 | async-start | bytes 6291456 | tf_op jit(solution)/shard_map/reduce_scatter | solution.py:234
  1444.8 33.0 %reduce-scatter.8.cloned.1.call-start = ((), (), s32[]{:S(2)}) async-start(), calls=%async_computation.9 | async-start | bytes 6291456 | tf_op jit(solution)/shard_map/reduce_scatter | solution.py:240
  (116 other events, 594.1 us)
Sparse Core Ops, SparseCore 0:
  1435.2 10.1 reduce-scatter.5
  1448.2 13.3 reduce-scatter.3
  1464.5 13.3 reduce-scatter.7
